TPU v7x, 512 devices: a whole 4x8x8 slice. The times are simulated.
512 devices in a mesh: tower: 8 (over z_hi, core), group: 4 (over x), blk: 16 (over y, z_lo).
Axes of the slice: x: 4, y: 8, z: 8 (z_hi: 4, z_lo: 2; z = z_hi * 2 + z_lo), core: 2. Of those that a mesh axis runs over, the one named last changes fastest.
Arguments:
- queries: bfloat16 [2048, 384, 256], P(('tower', 'group', 'blk')), may hold values from -102 to 102
- cluster_ids: int32 [2048, 64], P(('tower', 'group', 'blk')), may hold values from 0 to 127, all different within a row
- positives: int32 [2048, 384], P(('tower', 'group', 'blk')), may hold values from 0 to 1023
- owner_map: int32 [4, 128], P('group'), may hold values from 0 to 127, each once within a row
- panels: bfloat16 [512, 16, 256], P(('group', 'blk')), may hold values from -0.375 to 0.375
- scales: bfloat16 [512, 16], P(('group', 'blk')), may hold values from 0.5 to 2
Outputs:
- losses: bfloat16 [2048, 384], P(('tower', 'group', 'blk'))
- query_grads: bfloat16 [2048, 384, 256], P(('tower', 'group', 'blk'))
- panel_grads: float32 [512, 16, 256], P(('group', 'blk'), 'tower')
Inputs may be any that keep to these rules, and one draw needn't show every extreme that they name: `cluster_ids`: each row lists 64 different clusters. `owner_map`: each row is a permutation.
All inputs are finite; a program needn't handle non-finite values.
Results may differ from a plain program's by a relative error of at most 0.014.
Values may be sent and summed in bfloat16 or wider, within the bound.
A program may use at most 64 MiB of HBM per device.

v0:
```python
import jax
import jax.numpy as jnp
from jax import lax
from jax.sharding import PartitionSpec as P

FLOOR_SCORE = -1e30


def score_part(flat_query, panel_part, scale_part, row_sel, first_slot):
    how_many, panel_items, feat_width = panel_part.shape
    scale_row = scale_part.reshape(how_many * panel_items).astype(jnp.float32)
    scores = (
        jnp.dot(
            flat_query,
            panel_part.reshape(how_many * panel_items, feat_width).T,
            preferred_element_type=jnp.float32,
        )
        * scale_row[None, :]
    )
    allowed = jnp.repeat(row_sel, panel_items, axis=1)
    columns = first_slot * panel_items + lax.iota(jnp.int32, how_many * panel_items)
    return (scores, allowed, columns, scale_row)


def shards(queries, cluster_ids, positives, owner_map, panels, scales):
    queries, cluster_ids, positives = (
        lax.all_to_all(queries, "group", split_axis=0, concat_axis=0, tiled=True),
        lax.all_to_all(cluster_ids, "group", split_axis=0, concat_axis=0, tiled=True),
        lax.all_to_all(positives, "group", split_axis=0, concat_axis=0, tiled=True),
    )
    block_count, block_rows, feat_width = queries.shape
    per_dev, panel_items = scales.shape
    blk_count = lax.axis_size("blk")
    group_slots = per_dev * blk_count
    flat_query = queries.reshape(block_count * block_rows, feat_width)
    slot_iota = lax.iota(jnp.int32, group_slots)
    ids_hot = cluster_ids[:, :, None] == slot_iota[None, None, :]
    listed = jnp.sum(jnp.where(ids_hot, owner_map[0][None, None, :], 0), axis=2)
    selected = jnp.any(listed[:, :, None] == slot_iota[None, None, :], axis=1)
    row_sel = jnp.repeat(selected, block_rows, axis=0)
    pos_slot = jnp.take_along_axis(listed, positives // panel_items, axis=1)
    target = (pos_slot * panel_items + positives % panel_items).reshape(block_count * block_rows)
    row_total = block_count * block_rows
    whole_panels, whole_scales = (
        lax.all_gather(panels, "blk", axis=0, tiled=True),
        lax.all_gather(scales, "blk", axis=0, tiled=True),
    )
    peak_now = jnp.full((row_total,), FLOOR_SCORE, jnp.float32)
    scores, allowed, columns, scale_row = score_part(
        flat_query, whole_panels, whole_scales, row_sel, 0
    )
    masked = jnp.where(allowed, scores, FLOOR_SCORE)
    new_peak = jnp.maximum(peak_now, jnp.max(masked, axis=1))
    new_total = jnp.sum(jnp.where(allowed, jnp.exp(masked - new_peak[:, None]), 0.0), axis=1)
    pos_score = jnp.sum(jnp.where(columns[None, :] == target[:, None], scores, 0.0), axis=1)
    peak_now, total_now, pos_score = (new_peak, new_total, pos_score)
    log_total = peak_now + jnp.log(total_now)
    scores, allowed, columns, scale_row = score_part(
        flat_query, whole_panels, whole_scales, row_sel, 0
    )
    chances = jnp.where(allowed, jnp.exp(scores - log_total[:, None]), 0.0)
    is_target = (columns[None, :] == target[:, None]).astype(jnp.float32)
    weights = ((chances - is_target) * scale_row[None, :]).astype(jnp.bfloat16)
    query_acc = jnp.dot(
        weights,
        whole_panels.reshape(group_slots * panel_items, feat_width),
        preferred_element_type=jnp.float32,
    )
    grad_accum = lax.psum_scatter(
        jnp.dot(weights.T, flat_query, preferred_element_type=jnp.float32)
        .reshape(per_dev * lax.axis_size("blk"), panel_items, feat_width)
        .astype(jnp.bfloat16),
        "blk",
        scatter_dimension=0,
        tiled=True,
    )
    panel_grads = lax.psum_scatter(grad_accum, "tower", scatter_dimension=1, tiled=True).astype(
        jnp.float32
    )
    losses = (log_total - pos_score).astype(jnp.bfloat16).reshape(block_count, block_rows)
    query_grads = query_acc.astype(jnp.bfloat16).reshape(block_count, block_rows, feat_width)
    back_grads, back_losses = (
        lax.all_to_all(query_grads, "group", split_axis=0, concat_axis=0, tiled=True),
        lax.all_to_all(losses, "group", split_axis=0, concat_axis=0, tiled=True),
    )
    return (back_losses, back_grads, panel_grads)


def solution(mesh):
    return jax.shard_map(
        shards,
        mesh=mesh,
        in_specs=(
            P(("tower", "group", "blk"), None, None),
            P(("tower", "group", "blk"), None),
            P(("tower", "group", "blk"), None),
            P("group", None),
            P(("group", "blk"), None, None),
            P(("group", "blk"), None),
        ),
        out_specs=(
            P(("tower", "group", "blk"), None),
            P(("tower", "group", "blk"), None, None),
            P(("group", "blk"), "tower", None),
        ),
        check_vma=False,
    )
```

profile of v0, /device:TPU:1, one launch (start us, length us, event | category | flops | bytes accessed | tf_op | source)
XLA Modules:
  0.0 246.1 jit_solution(10100974512733483541)
XLA Ops:
  7.2 0.7 all-gather.2.cloned.1.call-update
  7.9 4.8 %all-to-all-start = ((s32[4,1,64]{2,1,0:T(1,128)}), s32[4,1,64]{2,1,0:T(1,128)S(1)}, u32[]{:S(2)}, u32[]{:S(2)}) async-start(s32[4,1,64]{2,1,0:T(1,128)} %bitcast.50), calls=%async_computation | async-start | bytes 4096 | tf_op jit(solution)/shard_map/all_to_all | solution.py:28
  12.7 0.7 all_to_all.31
  13.4 3.4 %all-to-all-done = s32[4,1,64]{2,1,0:T(1,128)S(1)} async-done(((s32[4,1,64]{2,1,0:T(1,128)}), s32[4,1,64]{2,1,0:T(1,128)S(1)}, u32[]{:S(2)}, u32[]{:S(2)}) %all-to-all-start) | async-done | bytes 1056 | tf_op jit(solution)/shard_map/all_to_all | solution.py:28
  16.8 6.5 %all_to_all.43 = s32[4,1,384]{2,1,0:T(1,128)S(1)} all-to-all(s32[4,1,384]{2,1,0:T(1,128)S(1)} %all_to_all.31), channel_id=1, replica_groups=mesh['tower'=8,'group'=4,'blk'=16] {'group'}, dimensions={0} | all-to-all | bytes 12288 | tf_op jit(solution)/shard_map/all_to_all | solution.py:29
  23.3 4.2 %all-to-all-start.1 = ((bf16[4,384,256]{2,1,0:T(8,128)(2,1)}), bf16[4,384,256]{2,1,0:T(8,128)(2,1)}, u32[]{:S(2)}, u32[]{:S(2)}) async-start(bf16[4,384,256]{2,1,0:T(8,128)(2,1)} %param.6), calls=%async_computation.1 | async-start | bytes 1572864 | tf_op jit(solution)/shard_map/all_to_all | solution.py:27
  27.5 29.4 %all_gather.7 = bf16[128,16]{1,0:T(8,128)(2,1)S(1)} all-gather(bf16[8,16]{1,0:T(8,128)(2,1)} %param.11), channel_id=1, replica_groups=mesh['tower'=8,'group'=4,'blk'=16] {'blk'}, dimensions={0}, use_global_device_ids=true | all-gather | bytes 4352 | tf_op jit(solution)/shard_map/all_gather | solution.py:46
  57.1 0.9 select_reduce_fusion.2
  58.5 0.8 broadcast_in_dim.52
  59.3 6.6 %copy.31 = pred[1536,2048]{1,0:T(32,128)(4,1)S(1)} copy(pred[1536,2048]{0,1:T(8,128)(4,1)S(1)} %bitcast.39) | data formatting | bytes 6291456 | tf_op jit(solution)/shard_map/reshape | solution.py:20
  66.1 13.3 %gather_fusion = s32[1536]{0:T(1024)S(1)} fusion(s32[4,64]{1,0:T(4,128)S(1)} %select_reduce_fusion.2, s32[1536]{0:T(1024)S(1)} %reshape.255), kind=kCustom, calls=%fused_computation | custom fusion | bytes 24576 | tf_op jit(solution)/shard_map/jit(take_along_axis)/gather | solution.py:41
  79.5 4.3 %fusion = (f32[1536]{0:T(1024)S(1)}, f32[1536,2048]{1,0:T(8,128)S(1)}) fusion(pred[1536,2048]{1,0:T(32,128)(4,1)S(1)} %copy.31, f32[2048]{0:T(1024)S(1)} %reshape.254, bf16[1536,256]{1,0:T(8,128)(2,1)} %bitcast.4, bf16[2048,256]{1,0:T(8,128)(2,1)} %bitcast.42), kind=kOutput, calls=%fused_computation.6 | convolution fusion | flops 1620048384 | bytes 17577984 | tf_op jit(solution)/shard_map/dot_general | solution.py:13
  83.8 7.2 %select_reduce_fusion = (f32[1536]{0:T(1024)S(1)}, f32[1536]{0:T(1024)S(1)}) fusion(f32[1536,2048]{1,0:T(8,128)S(1)} %get-tuple-element.23, s32[1536]{0:T(1024)S(1)} %fusion.2, f32[2048]{0:T(1024)S(1)} %reshape.254, pred[1536,2048]{1,0:T(32,128)(4,1)S(1)} %copy.31, f32[1536]{0:T(1024)S(1)} %broadcast_maximum_fusion), kind=kLoop, calls=%fused_computation.2 | loop fusion | flops 25162752 | bytes 15761408 | tf_op jit(solution)/shard_map/reduce_sum | solution.py:55
  91.0 6.8 %multiply_convert_fusion = bf16[1536,2048]{1,0:T(8,128)(2,1)} fusion(pred[1536,2048]{1,0:T(32,128)(4,1)S(1)} %copy.31, f32[1536,2048]{1,0:T(8,128)S(1)} %get-tuple-element.23, f32[1536]{0:T(1024)S(1)} %get-tuple-element.21, s32[1536]{0:T(1024)S(1)} %fusion.2, f32[2048]{0:T(1024)S(1)} %reshape.254), kind=kLoop, calls=%fused_computation.1 | loop fusion | flops 25165824 | bytes 22040576 | tf_op jit(solution)/shard_map/convert_element_type | solution.py:63
  97.8 8.6 %copy.35 = bf16[2048,1536]{1,0:T(8,128)(2,1)} copy(bf16[2048,1536]{0,1:T(8,128)(2,1)} %bitcast.38) | data formatting | bytes 12582912 | tf_op jit(solution)/shard_map/dot_general | solution.py:70
  106.5 4.8 %convolution_convert_fusion.1 = bf16[128,16,256]{2,1,0:T(8,128)(2,1)S(1)} fusion(bf16[128,16,1536]{2,1,0:T(8,128)(2,1)} %bitcast.40, bf16[1536,256,1]{1,0,2:T(8,128)(2,1)} %bitcast.10), kind=kOutput, calls=%fused_computation.8 | convolution fusion | flops 1611137024 | bytes 8126464 | tf_op jit(solution)/shard_map/dot_general | solution.py:70
  111.3 1.4 copy.42
  114.6 3.5 %all-to-all-start.3 = ((bf16[4,2,192]{2,1,0:T(2,128)(2,1)}), bf16[4,2,192]{2,1,0:T(2,128)(2,1)S(1)}, u32[]{:S(2)}, u32[]{:S(2)}) async-start(bf16[4,2,192]{2,1,0:T(2,128)(2,1)} %reshape.267), calls=%async_computation.3 | async-start | bytes 8192 | tf_op jit(solution)/shard_map/all_to_all | solution.py:84
  118.1 5.5 %convolution_convert_fusion = bf16[1536,256]{1,0:T(8,128)(2,1)} fusion(bf16[1536,2048]{1,0:T(8,128)(2,1)} %multiply_convert_fusion, bf16[2048,256]{1,0:T(8,128)(2,1)S(1)} %bitcast.43), kind=kOutput, calls=%fused_computation.7 | convolution fusion | flops 1611005952 | bytes 8126464 | tf_op jit(solution)/shard_map/dot_general | solution.py:64
  123.6 4.2 %all-to-all-start.4 = ((bf16[4,384,256]{2,1,0:T(8,128)(2,1)}), bf16[4,384,256]{2,1,0:T(8,128)(2,1)S(1)}, u32[]{:S(2)}, u32[]{:S(2)}) async-start(bf16[4,384,256]{2,1,0:T(8,128)(2,1)} %bitcast.7), calls=%async_computation.4 | async-start | bytes 1572864 | tf_op jit(solution)/shard_map/all_to_all | solution.py:83
  127.8 59.3 %reduce-scatter.7.cloned.1.call-done = bf16[8,4096]{1,0:T(8,128)(2,1)} async-done(((bf16[128,4096]{1,0:T(8,128)(2,1)}), bf16[8,4096]{1,0:T(8,128)(2,1)}) %reduce-scatter.7.cloned.1.call-update) | async-done | bytes 65552
  187.8 49.6 %reduce-scatter.5.cloned.1.call-done = bf16[8,2,256]{2,0,1:T(8,128)(2,1)} async-done(((bf16[8,16,256]{2,0,1:T(8,128)(2,1)}), bf16[8,2,256]{2,0,1:T(8,128)(2,1)}) %reduce-scatter.5.cloned.1.call-update) | async-done | bytes 8208 | tf_op jit(solution)/shard_map/reduce_scatter | solution.py:77
  237.4 1.3 copy.37
  238.7 0.9 copy.49
  (29 shorter events, 3.5 us)
Async XLA Ops:
  7.2 72.3 %all-gather.2.cloned.1.call-start = ((), (), s32[]{:S(2)}) async-start(), calls=%async_computation.7 | async-start | bytes 1114112 | tf_op jit(solution)/shard_map/all_gather | solution.py:45
  7.9 8.9 %all-to-all-start = ((s32[4,1,64]{2,1,0:T(1,128)}), s32[4,1,64]{2,1,0:T(1,128)S(1)}, u32[]{:S(2)}, u32[]{:S(2)}) async-start(s32[4,1,64]{2,1,0:T(1,128)} %bitcast.50), calls=%async_computation | async-start | bytes 4096 | tf_op jit(solution)/shard_map/all_to_all | solution.py:28
  23.3 56.2 %all-to-all-start.1 = ((bf16[4,384,256]{2,1,0:T(8,128)(2,1)}), bf16[4,384,256]{2,1,0:T(8,128)(2,1)}, u32[]{:S(2)}, u32[]{:S(2)}) async-start(bf16[4,384,256]{2,1,0:T(8,128)(2,1)} %param.6), calls=%async_computation.1 | async-start | bytes 1572864 | tf_op jit(solution)/shard_map/all_to_all | solution.py:27
  27.5 159.6 %reduce-scatter.7.cloned.1.call-start = ((), (), s32[]{:S(2)}) async-start(), calls=%async_computation.9 | async-start | bytes 1114112
  106.5 11.6 %copy-start = (bf16[128,16,256]{2,1,0:T(8,128)(2,1)S(1)}, bf16[128,16,256]{2,1,0:T(8,128)(2,1)}, u32[]{:S(2)}) copy-start(bf16[128,16,256]{2,1,0:T(8,128)(2,1)} %all-gather.2.cloned.1.call-done) | copy-start | bytes 3145732
  114.6 8.9 %all-to-all-start.3 = ((bf16[4,2,192]{2,1,0:T(2,128)(2,1)}), bf16[4,2,192]{2,1,0:T(2,128)(2,1)S(1)}, u32[]{:S(2)}, u32[]{:S(2)}) async-start(bf16[4,2,192]{2,1,0:T(2,128)(2,1)} %reshape.267), calls=%async_computation.3 | async-start | bytes 8192 | tf_op jit(solution)/shard_map/all_to_all | solution.py:84
  123.6 64.2 %all-to-all-start.4 = ((bf16[4,384,256]{2,1,0:T(8,128)(2,1)}), bf16[4,384,256]{2,1,0:T(8,128)(2,1)S(1)}, u32[]{:S(2)}, u32[]{:S(2)}) async-start(bf16[4,384,256]{2,1,0:T(8,128)(2,1)} %bitcast.7), calls=%async_computation.4 | async-start | bytes 1572864 | tf_op jit(solution)/shard_map/all_to_all | solution.py:83
  127.8 109.6 %reduce-scatter.5.cloned.1.call-start = ((), (), s32[]{:S(2)}) async-start(), calls=%async_computation.8 | async-start | bytes 73728 | tf_op jit(solution)/shard_map/reduce_scatter | solution.py:77
Sparse Core Ops, SparseCore 0:
  10.1 66.2 all-gather.1
  112.9 74.1 reduce-scatter.6
  189.9 47.4 reduce-scatter.4
where the time goes:
time: 248 us; the launch traced here: 246 us
  waiting for transfers between devices  113 us (46%)
  local copies, waits for them, and re-layouts  36.1 us (15%)
  blocking collectives  35.9 us (14%)
  starting transfers between devices  16.8 us (7%)
  other arithmetic  15.8 us (6%)
  matrix products  14.6 us (6%)
  between operations  13.9 us (6%)
    unnamed x4, waiting for transfers between devices  60 us
    reduce_scatter x1, waiting for transfers between devices, shards(): lax.psum_scatter(grad_accum, 'tower', scatter_dimension=1, tiled=True)  49.6 us
    all_gather x1, blocking collectives, shards(): lax.all_gather(scales, 'blk', axis=0, tiled=True)  29.4 us
    gather x2, local copies, waits for them, and re-layouts, shards(): pos_slot = jnp.take_along_axis(listed, positives // panel_items, axis=1)  13.3 us
    dot_general x1, local copies, waits for them, and re-layouts, shards(): jnp.dot(weights.T, flat_query, preferred_element_type=jnp.float32)  8.63 us
    reduce_sum x1, other arithmetic, shards(): jnp.sum(jnp.where(columns[None, :] == target[:, None], scores, 0.0), axis=1)  7.22 us
    convert_element_type x1, other arithmetic, shards(): weights = ((chances - is_target) * scale_row[None, :]).astype(jnp.bfloat16)  6.82 us
    reshape x1, local copies, waits for them, and re-layouts, score_part(): allowed = jnp.repeat(row_sel, panel_items, axis=1)  6.65 us
  transfers between devices with their start and end apart: 7, of which 3 were waited for; matrix products, arithmetic and copies ran while one was open for 12% of the time, Pallas kernels for 0%

commit v1 on v0

v1 whole, which is shorter than its diff:
```python
import functools

import jax
import jax.numpy as jnp
from jax import lax
from jax.experimental import pallas as pl
from jax.experimental.pallas import tpu as pltpu
from jax.sharding import PartitionSpec as P

MESH = pl.DeviceIdType.MESH
NX, NY, NZ = 4, 8, 8


def place():
    t, g, b = lax.axis_index("tower"), lax.axis_index("group"), lax.axis_index("blk")
    core, y = lax.rem(t, 2), lax.div(b, 2)
    z = 2 * lax.div(t, 2) + lax.rem(b, 2)
    return t, g, b, core, y, z


def at_yz(core, g, y, z):
    return (2 * lax.div(z, 2) + core, g, 2 * y + lax.rem(z, 2))


def barrier_with(peers):
    sem = pltpu.get_barrier_semaphore()
    for peer in peers:
        pl.semaphore_signal(sem, inc=1, device_id=peer, device_id_type=MESH)
    pl.semaphore_wait(sem, len(peers))


def remote(src, dst, send, recv, peer):
    return pltpu.make_async_remote_copy(
        src_ref=src, dst_ref=dst, send_sem=send, recv_sem=recv, device_id=peer, device_id_type=MESH
    )


def exchange_kernel(
    q, ids, pos, pan, sc,
    qo, ido, poso, pano, sco,
    loc, xs, xr, ys, yr, yss, yrs, zs, zr, zss, zrs, ps, pr,
):
    t, g, b, core, y, z = place()
    partner = (t + 1 - 2 * core, g, b)
    zl = lax.rem(z, 2)
    step = 1 - 2 * core
    z_to = at_yz(core, g, y, lax.rem(z + step + NZ, NZ))
    z_from = at_yz(core, g, y, lax.rem(z - step + NZ, NZ))
    x_peers = [(t, lax.rem(g + d, NX), b) for d in range(1, NX)]
    y_peers = [at_yz(core, g, lax.rem(y + d, NY), z) for d in range(1, NY)]
    local = [
        pltpu.make_async_copy(pan, pano.at[b], loc.at[0]),
        pltpu.make_async_copy(sc, sco.at[b], loc.at[1]),
        pltpu.make_async_copy(q.at[g], qo.at[g], loc.at[2]),
        pltpu.make_async_copy(ids.at[g], ido.at[g], loc.at[3]),
        pltpu.make_async_copy(pos.at[g], poso.at[g], loc.at[4]),
    ]
    for copy in local:
        copy.start()
    barrier_with(x_peers + y_peers + [z_to, z_from, partner])

    half = pl.ds(core * 4, 4)
    mine = pano.at[b, half]
    y_copies, z_copies, p_copies = [], [], []
    z_copies.append(remote(pan.at[half], mine, zs.at[0], zr.at[0], z_to))
    z_copies[0].start()
    z_scale = [remote(sc, sco.at[b], zss.at[0], zrs.at[0], z_to)]
    z_scale[0].start()
    y_scale = []
    for d in (4, 3, 5, 2, 6, 1, 7):
        y_copies.append((d, remote(pan.at[half], mine, ys.at[d - 1], yr.at[d - 1], y_peers[d - 1])))
        y_copies[-1][1].start()
        y_scale.append((d, remote(sc, sco.at[b], yss.at[d - 1], yrs.at[d - 1], y_peers[d - 1])))
        y_scale[-1][1].start()
    x_copies = []
    for d in (2, 1, 3):
        peer, dst = x_peers[d - 1], lax.rem(g + d, NX)
        for n, (src, out) in enumerate(((pos, poso), (ids, ido), (q, qo))):
            x_copies.append(remote(src.at[dst], out.at[g], xs.at[d - 1, n], xr.at[d - 1, n], peer))
            x_copies[-1].start()

    order = (1, 7, 2, 6, 3, 5, 4)
    by_d = dict(y_copies)
    scale_by_d = dict(y_scale)
    for n, d in enumerate(order):
        src = 2 * lax.rem(y - d + NY, NY) + zl
        piece = pano.at[src, half]
        by_d[d].wait_recv()
        z_copies.append(remote(piece, piece, zs.at[n + 1], zr.at[n + 1], z_to))
        z_copies[-1].start()
        p_copies.append(remote(piece, piece, ps.at[n], pr.at[n], partner))
        p_copies[-1].start()
        scale_by_d[d].wait_recv()
        z_scale.append(remote(sco.at[src], sco.at[src], zss.at[n + 1], zrs.at[n + 1], z_to))
        z_scale[-1].start()
    for n, d in enumerate((0,) + order):
        src = 2 * lax.rem(y - d + NY, NY) + 1 - zl
        piece = pano.at[src, half]
        z_copies[n].wait_recv()
        p_copies.append(remote(piece, piece, ps.at[7 + n], pr.at[7 + n], partner))
        p_copies[-1].start()
        z_scale[n].wait_recv()
    for copy in p_copies + x_copies:
        copy.wait_recv()
    for copy in local:
        copy.wait()
    for copy in [c for _, c in y_copies + y_scale] + z_copies + z_scale + p_copies + x_copies:
        copy.wait_send()


def compute_kernel(
    ids, owner, q_ref, pos_ref, pan_ref, sc_ref, qg_ref, loss_ref, grs_ref, tab, cand, sbuf, wbuf, acc
):
    items, sel = 16, ids.shape[2]
    rows = q_ref.shape[1]
    sub = lax.broadcasted_iota(jnp.int32, (items, rows), 0)
    eye = (
        lax.broadcasted_iota(jnp.int32, (items, items), 0)
        == lax.broadcasted_iota(jnp.int32, (items, items), 1)
    ).astype(jnp.float32)
    for n in range(sc_ref.shape[0]):
        part = sc_ref[n].astype(jnp.float32)
        column = jnp.sum(part[:, None, :] * eye[None], axis=2, keepdims=True)
        tab[pl.ds(8 * n, 8)] = jnp.broadcast_to(column, (8, items, 128))
    acc[...] = jnp.zeros_like(acc)

    def wide(slot):
        one = tab[slot]
        return jnp.concatenate([one] * (rows // 128), axis=1)

    def block(n, carry):
        slots = [owner[0, ids[n, 0, j]] for j in range(sel)]
        for j in range(sel):
            cand[pl.ds(items * j, items), :] = pan_ref[slots[j]]
        q = q_ref[n]
        sbuf[...] = lax.dot_general(
            cand[...], q, (((1,), (1,)), ((), ())), preferred_element_type=jnp.float32
        )
        peak = jnp.full((items, rows), -jnp.inf, jnp.float32)
        for j in range(sel):
            at = pl.ds(items * j, items)
            s = sbuf[at, :] * wide(slots[j])
            sbuf[at, :] = s
            peak = jnp.maximum(peak, s)
        peak = jnp.max(peak, axis=0, keepdims=True)
        pos = pos_ref[n]
        rel = jnp.broadcast_to(pos, (items, rows)) - sub
        total = jnp.zeros((items, rows), jnp.float32)
        picked = jnp.zeros((items, rows), jnp.float32)
        for j in range(sel):
            at = pl.ds(items * j, items)
            s = sbuf[at, :]
            picked = jnp.where(rel == items * j, s, picked)
            e = jnp.exp(s - peak)
            sbuf[at, :] = e
            total = total + e
        total = jnp.sum(total, axis=0, keepdims=True)
        picked = jnp.sum(picked, axis=0, keepdims=True)
        loss_ref[n] = peak + jnp.log(total) - picked
        inverse = 1.0 / total
        for j in range(sel):
            at = pl.ds(items * j, items)
            chance = sbuf[at, :] * inverse
            w = jnp.where(rel == items * j, chance - 1.0, chance) * wide(slots[j])
            wbuf[at, :] = w.astype(jnp.bfloat16)
        w = wbuf[...]
        grad = jnp.dot(w, q, preferred_element_type=jnp.float32)
        for j in range(sel):
            acc[slots[j]] += grad[items * j : items * (j + 1)]
        qg_ref[n] = lax.dot_general(
            w, cand[...], (((0,), (0,)), ((), ())), preferred_element_type=jnp.float32
        ).astype(jnp.bfloat16)
        return carry

    lax.fori_loop(0, q_ref.shape[0], block, 0)

    low = lax.broadcasted_iota(jnp.int32, (8, 256), 0) < 4

    def pack(y, carry):
        for zl in range(2):
            for h in range(2):
                base = (2 * y + zl) * 8 + 4 * h
                for v in range(2):
                    tiles = ([], [])
                    for sp in range(2):
                        a = acc[base + 2 * sp, 8 * v : 8 * v + 8, :]
                        c = acc[base + 2 * sp + 1, 8 * v : 8 * v + 8, :]
                        tiles[0].append(jnp.where(low, a, pltpu.roll(c, 4, axis=0)))
                        tiles[1].append(jnp.where(low, pltpu.roll(a, 4, axis=0), c))
                    for k in range(2):
                        z = 2 * (2 * v + k) + zl
                        tile = jnp.concatenate(tiles[k], axis=0).astype(jnp.bfloat16)
                        grs_ref[h, 0, y, z] = tile[:, :128]
                        grs_ref[h, 1, z, y] = tile[:, 128:]
        return carry

    lax.fori_loop(0, NY, pack, 0)


def reduce_kernel(
    grs, qg, loss_in, loss_out, qg_out, pg_out,
    r0, s0, r1, s1, r2, fin, rfin, lbuf,
    loc, cs, cr, fs, fr, s1s, s1r, s2s, s2r, xs, xr,
):
    t, g, b, core, y, z = place()
    partner = (t + 1 - 2 * core, g, b)
    x_peers = [(t, lax.rem(g + d, NX), b) for d in range(1, NX)]
    y_peers = [at_yz(core, g, lax.rem(y + d, NY), z) for d in range(1, NY)]
    z_peers = [at_yz(core, g, y, lax.rem(z + d, NZ)) for d in range(1, NZ)]
    local = [
        pltpu.make_async_copy(qg.at[g], qg_out.at[g], loc.at[0]),
        pltpu.make_async_copy(loss_in.at[g], lbuf.at[g], loc.at[1]),
    ]
    for copy in local:
        copy.start()
    barrier_with(x_peers + y_peers + z_peers + [partner])
    firsts = []
    for f in range(2):
        firsts.append(remote(grs.at[1 - core, f], r0.at[f], cs.at[f], cr.at[f], partner))
        firsts[f].start()
    backs = []
    for d in (2, 1, 3):
        peer, dst = x_peers[d - 1], lax.rem(g + d, NX)
        for n, (src, out) in enumerate(((loss_in, lbuf), (qg, qg_out))):
            backs.append(remote(src.at[dst], out.at[g], xs.at[d - 1, n], xr.at[d - 1, n], peer))
            backs[-1].start()
    here = (y, z)
    ahead = (y_peers, z_peers)
    stage1 = []
    for f in range(2):
        firsts[f].wait_recv()
        for k in range(NY):
            s0[f, k] = (
                grs[core, f, k].astype(jnp.float32) + r0[f, k].astype(jnp.float32)
            ).astype(jnp.bfloat16)
        for d in (4, 3, 5, 2, 6, 1, 7):
            copy = remote(
                s0.at[f, lax.rem(here[f] + d, 8)], r1.at[f, d - 1],
                s1s.at[f, d - 1], s1r.at[f, d - 1], ahead[f][d - 1],
            )
            copy.start()
            stage1.append(copy)
    stage2 = []
    for f in range(2):
        total = s0[f, here[f]].astype(jnp.float32)
        for copy in stage1[7 * f : 7 * f + 7]:
            copy.wait_recv()
        for d in range(7):
            total = total + r1[f, d].astype(jnp.float32)
        s1[f] = total.astype(jnp.bfloat16)
        for d in (4, 3, 5, 2, 6, 1, 7):
            copy = remote(
                s1.at[f, lax.rem(here[1 - f] + d, 8)], r2.at[f, d - 1],
                s2s.at[f, d - 1], s2r.at[f, d - 1], ahead[1 - f][d - 1],
            )
            copy.start()
            stage2.append(copy)
    for f in range(2):
        total = s1[f, here[1 - f]].astype(jnp.float32)
        for copy in stage2[7 * f : 7 * f + 7]:
            copy.wait_recv()
        for d in range(7):
            total = total + r2[f, d].astype(jnp.float32)
        fin[f] = total
    last = remote(fin, rfin, fs, fr, partner)
    last.start()
    for copy in local:
        copy.wait()
    for copy in backs:
        copy.wait_recv()
    for n in range(NX):
        loss_out[n : n + 1, :] = lbuf[n].astype(jnp.bfloat16)
    last.wait_recv()
    for h in range(2):
        for f in range(2):
            tile = jnp.where(core == h, fin[f], rfin[f])
            for k in range(4):
                rows = jnp.where(core == 0, tile[4 * k : 4 * k + 2], tile[4 * k + 2 : 4 * k + 4])
                pg_out[4 * h + k, :, 128 * f : 128 * f + 128] = rows
    for copy in firsts + stage1 + stage2 + backs + [last]:
        copy.wait_send()


def shards(queries, cluster_ids, positives, owner_map, panels, scales):
    count, rows, width = queries.shape
    slots, items = scales.shape
    blks = lax.axis_size("blk")
    sel = cluster_ids.shape[1]
    dma = pltpu.SemaphoreType.DMA
    anyspec = pl.BlockSpec(memory_space=pl.ANY)
    vmem = pl.BlockSpec(memory_space=pltpu.VMEM)
    smem = pl.BlockSpec(memory_space=pltpu.SMEM)
    f32, bf16, i32 = jnp.float32, jnp.bfloat16, jnp.int32
    sds = jax.ShapeDtypeStruct

    q_all, ids_all, pos_all, pan_all, sc_all = pl.pallas_call(
        exchange_kernel,
        out_shape=(
            sds((count, rows, width), bf16),
            sds((count, 1, sel), i32),
            sds((count, 1, rows), i32),
            sds((blks, slots, items, width), bf16),
            sds((blks, slots, items), bf16),
        ),
        in_specs=[anyspec] * 5,
        out_specs=(vmem,) * 5,
        scratch_shapes=[
            dma((5,)), dma((3, 3)), dma((3, 3)), dma((7,)), dma((7,)), dma((7,)), dma((7,)),
            dma((8,)), dma((8,)), dma((8,)), dma((8,)), dma((15,)), dma((15,)),
        ],
        compiler_params=pltpu.CompilerParams(
            collective_id=0, has_side_effects=True, vmem_limit_bytes=8 << 20
        ),
        name="exchange",
    )(queries, cluster_ids.reshape(count, 1, sel), positives.reshape(count, 1, rows), panels, scales)

    qg, loss, grs = pl.pallas_call(
        compute_kernel,
        out_shape=(
            sds((count, rows, width), bf16),
            sds((count, 1, rows), f32),
            sds((2, 2, 8, 8, 16, 128), bf16),
        ),
        in_specs=[smem, smem, vmem, vmem, vmem, vmem],
        out_specs=(vmem,) * 3,
        scratch_shapes=[
            pltpu.VMEM((blks * slots, items, 128), f32),
            pltpu.VMEM((sel * items, width), bf16),
            pltpu.VMEM((sel * items, rows), f32),
            pltpu.VMEM((sel * items, rows), bf16),
            pltpu.VMEM((blks * slots, items, width), f32),
        ],
        compiler_params=pltpu.CompilerParams(vmem_limit_bytes=24 << 20),
        name="score",
    )(ids_all, owner_map, q_all, pos_all, pan_all.reshape(blks * slots, items, width), sc_all)

    return pl.pallas_call(
        reduce_kernel,
        out_shape=(
            sds((count, rows), bf16),
            sds((count, rows, width), bf16),
            sds((slots, 2, width), f32),
        ),
        in_specs=[vmem, vmem, vmem],
        out_specs=(vmem, anyspec, vmem),
        scratch_shapes=[
            pltpu.VMEM((2, 8, 8, 16, 128), bf16),
            pltpu.VMEM((2, 8, 8, 16, 128), bf16),
            pltpu.VMEM((2, 7, 8, 16, 128), bf16),
            pltpu.VMEM((2, 8, 16, 128), bf16),
            pltpu.VMEM((2, 7, 16, 128), bf16),
            pltpu.VMEM((2, 16, 128), f32),
            pltpu.VMEM((2, 16, 128), f32),
            pltpu.VMEM((count, 1, rows), f32),
            dma((2,)), dma((2,)), dma((2,)), dma, dma, dma((2, 7)), dma((2, 7)), dma((2, 7)), dma((2, 7)),
            dma((3, 2)), dma((3, 2)),
        ],
        compiler_params=pltpu.CompilerParams(
            collective_id=1, has_side_effects=True, vmem_limit_bytes=16 << 20
        ),
        name="reduce",
    )(grs, qg, loss)


def solution(mesh):
    return jax.shard_map(
        shards,
        mesh=mesh,
        in_specs=(
            P(("tower", "group", "blk"), None, None),
            P(("tower", "group", "blk"), None),
            P(("tower", "group", "blk"), None),
            P("group", None),
            P(("group", "blk"), None, None),
            P(("group", "blk"), None),
        ),
        out_specs=(
            P(("tower", "group", "blk"), None),
            P(("tower", "group", "blk"), None, None),
            P(("group", "blk"), "tower", None),
        ),
        check_vma=False,
    )
```

time: 248 us -> 66 us (0.27)
  waiting for transfers between devices: 113 us -> 0 us
  Pallas kernels: 0 us -> 59.6 us
  blocking collectives: 35.9 us -> 0 us
  local copies, waits for them, and re-layouts: 36.1 us -> 5.4 us
  starting transfers between devices: 16.8 us -> 0 us
  other arithmetic: 15.8 us -> 0 us
  matrix products: 14.6 us -> 0 us
  between operations: 13.9 us -> 0.69 us
    unnamed x4 -> x0, waiting for transfers between devices: 60 us -> none
    pallas_call x0 -> x3, Pallas kernels: none -> 59.6 us  [the longest x1 30.1 us: shards(): pl.pallas_call(exchange_kernel, out_shape=(sds((count, rows, width), bf16...]
    reduce_scatter x1 -> x0, waiting for transfers between devices: 49.6 us -> none  [shards(): lax.psum_scatter(grad_accum, 'tower', scatter_dimension=1, tiled=True)]
    all_gather x1 -> x0, blocking collectives: 29.4 us -> none  [shards(): lax.all_gather(scales, 'blk', axis=0, tiled=True)]
    all_to_all x4 -> x0, starting transfers between devices: 16.7 us -> none  [the longest x1 4.84 us: shards(): lax.all_to_all(cluster_ids, 'group', split_axis=0, concat_axis=0, tiled=T...]
    dot_general x3 -> x0, matrix products: 14.6 us -> none  [the longest x1 5.47 us: shards(): jnp.dot(weights, whole_panels.reshape(group_slots * panel_items, feat_wid...]
    gather x2 -> x0, local copies, waits for them, and re-layouts: 13.3 us -> none  [shards(): pos_slot = jnp.take_along_axis(listed, positives // panel_items, axis=1)]
    dot_general x1 -> x0, local copies, waits for them, and re-layouts: 8.63 us -> none  [shards(): jnp.dot(weights.T, flat_query, preferred_element_type=jnp.float32)]
  transfers between devices with their start and end apart: 7 -> 0, of which waited for: 3 -> 0; matrix products, arithmetic and copies ran while one was open for 12% -> 0% of each run, Pallas kernels for 0% -> 0%
where the time goes in v1:
time: 66 us; the launch traced here: 65.7 us
  Pallas kernels  59.6 us (90%)
  local copies, waits for them, and re-layouts  5.4 us (8%)
  between operations  0.69 us (1%)
    pallas_call x1, Pallas kernels, shards(): pl.pallas_call(exchange_kernel, out_shape=(sds((count, rows, width), bf16...  30.1 us
    pallas_call x1, Pallas kernels, shards(): pl.pallas_call(reduce_kernel, out_shape=(sds((count, rows), bf16), sds((c...  20.8 us
    pallas_call x1, Pallas kernels, shards(): pl.pallas_call(compute_kernel, out_shape=(sds((count, rows, width), bf16)...  8.67 us
    unnamed x13, local copies, waits for them, and re-layouts  4.69 us

profile of v1, /device:TPU:1, one launch (start us, length us, event | category | flops | bytes accessed | tf_op | source)
XLA Modules:
  0.0 65.7 jit_solution(5511449949011009025)
XLA Ops:
  0.6 0.0 copy-start.2
  0.6 0.0 copy-start.3
  0.7 0.7 %reshape.16.pos = s32[4,1,384]{2,1,0:T(1,128)S(1)} reshape(s32[4,384]{1,0:T(4,128)} %param.8) | data formatting | bytes 12288 | tf_op jit(solution)/shard_map/reshape | solution.py:315
  1.4 0.0 copy-done.2
  1.4 0.0 copy-done.3
  1.4 0.0 copy-start
  1.4 1.1 %copy-done = bf16[4,384,256]{2,1,0:T(8,128)(2,1)S(1)} copy-done((bf16[4,384,256]{2,1,0:T(8,128)(2,1)S(1)}, bf16[4,384,256]{2,1,0:T(8,128)(2,1)}, u32[]{:S(2)}) %copy-start) | copy-done | bytes 786456
  2.5 0.0 copy-start.1
  2.5 0.8 %copy-done.1 = bf16[8,16,256]{2,1,0:T(8,128)(2,1)S(1)} copy-done((bf16[8,16,256]{2,1,0:T(8,128)(2,1)S(1)}, bf16[8,16,256]{2,1,0:T(8,128)(2,1)}, u32[]{:S(2)}) %copy-start.1) | copy-done | bytes 65560
  3.3 30.1 %exchange.1 = (bf16[4,384,256]{2,1,0:T(8,128)(2,1)S(1)}, s32[4,1,64]{2,1,0:T(1,128)S(1)}, s32[4,1,384]{2,1,0:T(1,128)S(1)}, bf16[16,8,16,256]{3,2,1,0:T(8,128)(2,1)S(1)}, bf16[16,8,16]{2,1,0:T(8,128)(2,1)S(1)}) custom-call(bf16[4,384,256]{2,1,0:T(8,128)(2,1)S(1)} %copy-done, s32[4,1,64]{2,1,0:T(1,128)S(1)} %bitcast.3, s32[4,1,384]{2,1,0:T(1,128)S(1)} %reshape.16.pos, ...), custom_call_target="tpu_custom_call" | custom-call | tf_op jit(solution)/shard_map/exchange/pallas_call | solution.py:296
  33.5 0.0 copy-start.4
  33.5 0.6 copy-done.4
  34.1 8.7 %score.1 = (bf16[4,384,256]{2,1,0:T(8,128)(2,1)S(1)}, f32[4,1,384]{2,1,0:T(1,128)S(1)}, bf16[2,2,8,8,16,128]{5,4,3,2,1,0:T(8,128)(2,1)S(1)}) custom-call(s32[4,1,64]{2,1,0:T(1,128)S(1)} %get-tuple-element.11.ids, s32[1,128]{1,0:T(1,128)S(1)} %copy-done.4, bf16[4,384,256]{2,1,0:T(8,128)(2,1)S(1)} %get-tuple-element.12.q_ref, ...), custom_call_target="tpu_custom_call" | custom-call | tf_op jit(solution)/shard_map/score/pallas_call | solution.py:317
  42.8 20.8 %reduce.1 = (bf16[4,384]{1,0:T(4,128)(2,1)S(1)}, bf16[4,384,256]{2,1,0:T(8,128)(2,1)S(1)}, f32[8,2,256]{2,1,0:T(2,128)S(1)}) custom-call(bf16[2,2,8,8,16,128]{5,4,3,2,1,0:T(8,128)(2,1)S(1)} %get-tuple-element.16.grs, bf16[4,384,256]{2,1,0:T(8,128)(2,1)S(1)} %get-tuple-element.17.qg, f32[4,1,384]{2,1,0:T(1,128)S(1)} %get-tuple-element.18.loss_in), custom_call_target="tpu_custom_call" | custom-call | tf_op jit(solution)/shard_map/reduce/pallas_call | solution.py:337
  63.6 0.6 copy.12
  64.2 0.9 %copy.13 = bf16[4,384,256]{2,1,0:T(8,128)(2,1)} copy(bf16[4,384,256]{2,1,0:T(8,128)(2,1)S(1)} %get-tuple-element.23) | data formatting | bytes 1572864
  65.1 0.6 copy.14
Async XLA Ops:
  0.6 0.7 %copy-start.2 = (s32[4,64]{1,0:T(4,128)S(1)}, s32[4,64]{1,0:T(4,128)}, u32[]{:S(2)}) copy-start(s32[4,64]{1,0:T(4,128)} %param.7) | copy-start | bytes 3076
  0.6 0.7 %copy-start.3 = (bf16[8,16]{1,0:T(8,128)(2,1)S(1)}, bf16[8,16]{1,0:T(8,128)(2,1)}, u32[]{:S(2)}) copy-start(bf16[8,16]{1,0:T(8,128)(2,1)} %sc.1) | copy-start | bytes 772
  1.4 1.1 %copy-start = (bf16[4,384,256]{2,1,0:T(8,128)(2,1)S(1)}, bf16[4,384,256]{2,1,0:T(8,128)(2,1)}, u32[]{:S(2)}) copy-start(bf16[4,384,256]{2,1,0:T(8,128)(2,1)} %q.1) | copy-start | bytes 2359300
  2.5 0.8 %copy-start.1 = (bf16[8,16,256]{2,1,0:T(8,128)(2,1)S(1)}, bf16[8,16,256]{2,1,0:T(8,128)(2,1)}, u32[]{:S(2)}) copy-start(bf16[8,16,256]{2,1,0:T(8,128)(2,1)} %pan.1) | copy-start | bytes 196612
  33.5 0.7 %copy-start.4 = (s32[1,128]{1,0:T(1,128)S(1)}, s32[1,128]{1,0:T(1,128)}, u32[]{:S(2)}) copy-start(s32[1,128]{1,0:T(1,128)} %owner.1) | copy-start | bytes 1540

commit v2 on v0

v2 whole, which is shorter than its diff:
```python
import jax
import jax.numpy as jnp
from jax import lax
from jax.experimental import pallas as pl
from jax.experimental.pallas import tpu as pltpu
from jax.sharding import PartitionSpec as P

MESH = pl.DeviceIdType.MESH
NX, NY, NZ = 4, 8, 8
FAR_FIRST = (4, 3, 5, 2, 6, 1, 7)


def remote(src, dst, send, recv, peer):
    return pltpu.make_async_remote_copy(
        src_ref=src, dst_ref=dst, send_sem=send, recv_sem=recv, device_id=peer, device_id_type=MESH
    )


def signal(sem, peer):
    pl.semaphore_signal(sem, inc=1, device_id=peer, device_id_type=MESH)


def score_block(n, row, slots, q_ref, pos_ref, pan_ref, tab, cand, sbuf, wbuf, gbuf, loss_ref):
    items, sel, rows = 16, len(slots), q_ref.shape[1]
    sub = lax.broadcasted_iota(jnp.int32, (items, rows), 0)

    def wide(slot):
        one = tab[slot]
        return jnp.concatenate([one] * (rows // 128), axis=1)

    for j in range(sel):
        cand[n, pl.ds(items * j, items), :] = pan_ref[slots[j]]
    q = q_ref[n]
    sbuf[...] = lax.dot_general(
        cand[n], q, (((1,), (1,)), ((), ())), preferred_element_type=jnp.float32
    )
    peak = jnp.full((items, rows), -jnp.inf, jnp.float32)
    for j in range(sel):
        at = pl.ds(items * j, items)
        s = sbuf[at, :] * wide(slots[j])
        sbuf[at, :] = s
        peak = jnp.maximum(peak, s)
    peak = jnp.max(peak, axis=0, keepdims=True)
    pos = pos_ref[n, pl.ds(row, 1), :]
    rel = jnp.broadcast_to(pos, (items, rows)) - sub
    total = jnp.zeros((items, rows), jnp.float32)
    picked = jnp.zeros((items, rows), jnp.float32)
    for j in range(sel):
        at = pl.ds(items * j, items)
        s = sbuf[at, :]
        picked = jnp.where(rel == items * j, s, picked)
        e = jnp.exp(s - peak)
        sbuf[at, :] = e
        total = total + e
    total = jnp.sum(total, axis=0, keepdims=True)
    picked = jnp.sum(picked, axis=0, keepdims=True)
    loss_ref[n] = peak + jnp.log(total) - picked
    inverse = 1.0 / total
    for j in range(sel):
        at = pl.ds(items * j, items)
        chance = sbuf[at, :] * inverse
        w = jnp.where(rel == items * j, chance - 1.0, chance) * wide(slots[j])
        wbuf[n, at, :] = w.astype(jnp.bfloat16)
    grad = jnp.dot(wbuf[n], q, preferred_element_type=jnp.float32)
    gbuf[n, pl.ds(0, sel)] = grad.reshape(sel, items, grad.shape[1])


def main_kernel(
    owner, q, ids, pos, pan, sc,
    qg_out, loss_out, fin_out, rfin,
    qo, ido, poso, pano, sco, ids_s, tab, cand, sbuf, wbuf, gbuf, lossb, qgb, inv_v, inv_s,
    p0, own0, r0, s0, r1, s1, r2, fin,
    loc, xs, xr, ys, yr, yss, yrs, zs, zr, zss, zrs, ps, pr, ready1, ready2,
    cs, cr, s1s, s1r, s2s, s2r, bs, br, fs, fr,
):
    t, g, b = lax.axis_index("tower"), lax.axis_index("group"), lax.axis_index("blk")
    core, y, zl = lax.rem(t, 2), lax.div(b, 2), lax.rem(b, 2)
    z = 2 * lax.div(t, 2) + zl
    step = 1 - 2 * core

    def at_yz(yy, zz):
        yy, zz = lax.rem(yy + NY, NY), lax.rem(zz + NZ, NZ)
        return (2 * lax.div(zz, 2) + core, g, 2 * yy + lax.rem(zz, 2))

    partner = (t + step, g, b)
    x_peers = [(t, lax.rem(g + d, NX), b) for d in range(1, NX)]
    z_to, z_from = at_yz(y, z + step), at_yz(y, z - step)

    local = [
        pltpu.make_async_copy(pan, pano.at[b], loc.at[0]),
        pltpu.make_async_copy(sc, sco.at[b], loc.at[1]),
        pltpu.make_async_copy(q.at[g], qo.at[g], loc.at[2]),
        pltpu.make_async_copy(ids.at[g], ido.at[g], loc.at[3]),
        pltpu.make_async_copy(pos, poso.at[g], loc.at[4]),
    ]
    near = [at_yz(y + d, z) for d in (2, -2, 1, -1)] + x_peers + [z_to, z_from, partner]
    barrier = pltpu.get_barrier_semaphore()
    for peer in near:
        signal(barrier, peer)
    for copy in local:
        copy.start()
    pl.semaphore_wait(barrier, len(near))
    for peer in (z_to, z_from):
        signal(ready1, peer)

    half = pl.ds(core * 4, 4)
    sends = []

    def send(src, dst, s, r, peer):
        copy = remote(src, dst, s, r, peer)
        copy.start()
        sends.append(copy)
        return copy

    y_in, z_in, p_in = {}, {}, []

    def y_send(d, src_blk, to_y):
        for own, (buf, s, r) in (
            (pan.at[half], (pano.at[src_blk, half], ys, yr)),
            (sc, (sco.at[src_blk], yss, yrs)),
        ):
            src = own if src_blk is b else buf
            y_in.setdefault(d, []).append(send(src, buf, s.at[d - 1], r.at[d - 1], at_yz(to_y, z)))

    def z_send(d, src_blk):
        for own, (buf, s, r) in (
            (pan.at[half], (pano.at[src_blk, half], zs, zr)),
            (sc, (sco.at[src_blk], zss, zrs)),
        ):
            src = own if src_blk is b else buf
            z_in.setdefault(d, []).append(send(src, buf, s.at[d], r.at[d], z_to))

    def p_send(src_blk):
        k = len(p_in)
        piece = pano.at[src_blk, half]
        p_in.append(send(piece, piece, ps.at[k], pr.at[k], partner))

    def blk_at(d, side):
        return 2 * lax.rem(y - d + NY, NY) + side

    y_send(2, b, y + 2)
    y_send(6, b, y - 2)
    y_send(1, b, y + 1)
    y_send(7, b, y - 1)
    z_send(0, b)
    x_in = []
    for d in (2, 1, 3):
        dst = lax.rem(g + d, NX)
        for n, (src, out) in enumerate(
            ((ids.at[dst], ido.at[g]), (pos, poso.at[g]), (q.at[dst], qo.at[g]))
        ):
            x_in.append(send(src, out, xs.at[d - 1, n], xr.at[d - 1, n], x_peers[d - 1]))

    def take_y(d):
        for copy in y_in[d]:
            copy.wait_recv()

    def take_z(d):
        for copy in z_in[d]:
            copy.wait_recv()
        p_send(blk_at(d, 1 - zl))

    for d in (1, 7):
        take_y(d)
        z_send(d, blk_at(d, zl))
        p_send(blk_at(d, zl))
    take_y(2)
    y_send(3, blk_at(2, zl), y + 1)
    take_y(6)
    y_send(5, blk_at(6, zl), y - 1)
    y_send(4, 2 * lax.rem(y - 2 * step + NY, NY) + zl, y + 2 * step)
    for d in (2, 6):
        z_send(d, blk_at(d, zl))
        p_send(blk_at(d, zl))
    take_z(0)
    pl.semaphore_wait(ready1, 2)
    for d in (2, -2):
        signal(ready2, at_yz(y, z + d))
    take_z(1)
    take_z(7)
    for d in (3, 5, 4):
        take_y(d)
        z_send(d, blk_at(d, zl))
        p_send(blk_at(d, zl))
    for d in (2, 6, 3, 5, 4):
        take_z(d)
    for copy in local:
        copy.wait()
    for copy in x_in:
        copy.wait_recv()
    to_smem = pltpu.make_async_copy(ido, ids_s, loc.at[5])
    to_smem.start()

    items = 16
    eye = (
        lax.broadcasted_iota(jnp.int32, (items, items), 0)
        == lax.broadcasted_iota(jnp.int32, (items, items), 1)
    ).astype(jnp.float32)
    for n in range(sco.shape[0]):
        part = sco[n].astype(jnp.float32)
        column = jnp.sum(part[:, None, :] * eye[None], axis=2, keepdims=True)
        tab[pl.ds(8 * n, 8)] = jnp.broadcast_to(column, (8, items, 128))
    sel = ids_s.shape[2]
    for n in range(NX):
        gbuf[n, sel] = jnp.zeros(gbuf.shape[2:], jnp.float32)
    for copy in p_in:
        copy.wait_recv()
    to_smem.wait()
    lane = lax.broadcasted_iota(jnp.int32, (1, 128), 1)

    def block(n, carry):
        slots = [owner[0, ids_s[n, 0, j]] for j in range(sel)]
        where = jnp.full((1, 128), sel, jnp.int32)
        for j in range(sel):
            where = jnp.where(lane == slots[j], j, where)
        inv_v[n] = where
        score_block(n, g, slots, qo, poso, panf(pano), tab, cand, sbuf, wbuf, gbuf, lossb)
        return carry

    lax.fori_loop(0, NX, block, 0)
    inv_copy = pltpu.make_async_copy(inv_v, inv_s, loc.at[6])
    inv_copy.start()
    inv_copy.wait()

    low = lax.broadcasted_iota(jnp.int32, (8, 256), 0) < 4

    def pack(h, out, yy):
        for side in range(2):
            base = (2 * yy + side) * 8 + 4 * h
            rows = []
            for k in range(4):
                total = gbuf[0, inv_s[0, 0, base + k]]
                for n in range(1, NX):
                    total = total + gbuf[n, inv_s[n, 0, base + k]]
                rows.append(total)
            for v in range(2):
                tiles = ([], [])
                for sp in range(2):
                    a = rows[2 * sp][8 * v : 8 * v + 8]
                    c = rows[2 * sp + 1][8 * v : 8 * v + 8]
                    tiles[0].append(jnp.where(low, a, pltpu.roll(c, 4, axis=0)))
                    tiles[1].append(jnp.where(low, pltpu.roll(a, 4, axis=0), c))
                for k in range(2):
                    zz = 2 * (2 * v + k) + side
                    tile = jnp.concatenate(tiles[k], axis=0).astype(out.dtype)
                    out[0, yy, zz] = tile[:, :128]
                    out[1, zz, yy] = tile[:, 128:]

    def pack_away(yy, carry):
        pack(1 - core, p0, yy)
        return carry

    def pack_own(yy, carry):
        pack(core, own0, yy)
        return carry

    firsts = []
    lax.fori_loop(0, NY, pack_away, 0)
    for f in range(2):
        firsts.append(send(p0.at[f], r0.at[f], cs.at[f], cr.at[f], partner))
    lax.fori_loop(0, NY, pack_own, 0)
    pl.semaphore_wait(ready2, 2)
    here = (y, z)
    ahead = (lambda d: at_yz(y + d, z), lambda d: at_yz(y, z + d))
    stage1 = ([], [])

    for f in range(2):
        firsts[f].wait_recv()
    for d in FAR_FIRST + (0,):
        for f in range(2):
            k = lax.rem(here[f] + d, 8)
            s0[f, k] = (own0[f, k] + r0[f, k].astype(jnp.float32)).astype(jnp.bfloat16)
            if d:
                stage1[f].append(
                    send(s0.at[f, k], r1.at[f, d - 1], s1s.at[f, d - 1], s1r.at[f, d - 1], ahead[f](d))
                )

    def back(n, carry):
        qgb[n] = lax.dot_general(
            wbuf[n], cand[n], (((0,), (0,)), ((), ())), preferred_element_type=jnp.float32
        ).astype(jnp.bfloat16)
        return carry

    lax.fori_loop(0, NX, back, 0)
    home = [
        pltpu.make_async_copy(qgb.at[g], qg_out.at[g], loc.at[7]),
        pltpu.make_async_copy(lossb.at[g], loss_out.at[g], loc.at[8]),
    ]
    backs = []
    for d in (2, 1, 3):
        dst = lax.rem(g + d, NX)
        for n, (src, out) in enumerate(((lossb, loss_out), (qgb, qg_out))):
            backs.append(send(src.at[dst], out.at[g], bs.at[d - 1, n], br.at[d - 1, n], x_peers[d - 1]))
    for copy in home:
        copy.start()

    stage2 = ([], [])
    for f in range(2):
        for copy in stage1[f]:
            copy.wait_recv()
        total = s0[f, here[f]].astype(jnp.float32)
        for d in range(7):
            total = total + r1[f, d].astype(jnp.float32)
        s1[f] = total.astype(jnp.bfloat16)
        for d in FAR_FIRST:
            k = lax.rem(here[1 - f] + d, 8)
            stage2[f].append(
                send(s1.at[f, k], r2.at[f, d - 1], s2s.at[f, d - 1], s2r.at[f, d - 1], ahead[1 - f](d))
            )
    for f in range(2):
        for copy in stage2[f]:
            copy.wait_recv()
        total = s1[f, here[1 - f]].astype(jnp.float32)
        for d in range(7):
            total = total + r2[f, d].astype(jnp.float32)
        fin[f] = total
    last = send(fin, rfin, fs, fr, partner)
    home.append(pltpu.make_async_copy(fin, fin_out, loc.at[9]))
    home[-1].start()
    for copy in home:
        copy.wait()
    for copy in backs:
        copy.wait_recv()
    last.wait_recv()
    for copy in sends:
        copy.wait_send()


def panf(ref):
    return ref.reshape(ref.shape[0] * ref.shape[1], *ref.shape[2:])


def output_kernel(qg, loss, fin, rfin, loss_out, qg_out, pg_out, qv, lv, fv, rv, lossv, pgv, sem):
    small = [
        pltpu.make_async_copy(src, dst, sem.at[n])
        for n, (src, dst) in enumerate(((loss, lv), (fin, fv), (rfin, rv)))
    ]
    taken = [pltpu.make_async_copy(qg.at[n], qv.at[n], sem.at[3 + n]) for n in range(NX)]
    for copy in small + taken:
        copy.start()
    given = []
    for copy in small:
        copy.wait()
    core = lax.rem(lax.axis_index("tower"), 2)
    for n in range(NX):
        lossv[n : n + 1, :] = lv[n].astype(jnp.bfloat16)
    for h in range(2):
        for f in range(2):
            tile = jnp.where(core == h, fv[f], rv[f])
            for k in range(4):
                rows = jnp.where(core == 0, tile[4 * k : 4 * k + 2], tile[4 * k + 2 : 4 * k + 4])
                pgv[4 * h + k, :, 128 * f : 128 * f + 128] = rows
    given = [
        pltpu.make_async_copy(lossv, loss_out, sem.at[7]),
        pltpu.make_async_copy(pgv, pg_out, sem.at[8]),
    ]
    for copy in given:
        copy.start()
    for n in range(NX):
        taken[n].wait()
        given.append(pltpu.make_async_copy(qv.at[n], qg_out.at[n], sem.at[9 + n]))
        given[-1].start()
    for copy in given:
        copy.wait()


def shards(queries, cluster_ids, positives, owner_map, panels, scales):
    count, rows, width = queries.shape
    slots, items = scales.shape
    blks = lax.axis_size("blk")
    sel = cluster_ids.shape[1]
    dma = pltpu.SemaphoreType.DMA
    hbm = pl.BlockSpec(memory_space=pltpu.HBM)
    vmem = pl.BlockSpec(memory_space=pltpu.VMEM)
    smem = pl.BlockSpec(memory_space=pltpu.SMEM)
    f32, bf16, i32 = jnp.float32, jnp.bfloat16, jnp.int32
    sds = jax.ShapeDtypeStruct
    vm = pltpu.VMEM

    qg, loss, fin, rfin = pl.pallas_call(
        main_kernel,
        out_shape=(
            sds((count, rows, width), bf16),
            sds((count, 1, rows), f32),
            sds((2, 16, 128), f32),
            sds((2, 16, 128), f32),
        ),
        in_specs=[smem] + [hbm] * 5,
        out_specs=(hbm,) * 4,
        scratch_shapes=[
            vm((count, rows, width), bf16),
            vm((count, 1, sel), i32),
            vm((count, count, rows), i32),
            vm((blks, slots, items, width), bf16),
            vm((blks, slots, items), bf16),
            pltpu.SMEM((count, 1, sel), i32),
            vm((blks * slots, items, 128), f32),
            vm((count, sel * items, width), bf16),
            vm((sel * items, rows), f32),
            vm((count, sel * items, rows), bf16),
            vm((count, sel + 1, items, width), f32),
            vm((count, 1, rows), f32),
            vm((count, rows, width), bf16),
            vm((count, 1, 128), i32),
            pltpu.SMEM((count, 1, 128), i32),
            vm((2, 8, 8, 16, 128), bf16),
            vm((2, 8, 8, 16, 128), f32),
            vm((2, 8, 8, 16, 128), bf16),
            vm((2, 8, 8, 16, 128), bf16),
            vm((2, 7, 8, 16, 128), bf16),
            vm((2, 8, 16, 128), bf16),
            vm((2, 7, 16, 128), bf16),
            vm((2, 16, 128), f32),
            dma((10,)), dma((3, 3)), dma((3, 3)),
            dma((7,)), dma((7,)), dma((7,)), dma((7,)),
            dma((8,)), dma((8,)), dma((8,)), dma((8,)), dma((15,)), dma((15,)),
            pltpu.SemaphoreType.REGULAR, pltpu.SemaphoreType.REGULAR,
            dma((2,)), dma((2,)), dma((2, 7)), dma((2, 7)), dma((2, 7)), dma((2, 7)),
            dma((3, 2)), dma((3, 2)), dma, dma,
        ],
        compiler_params=pltpu.CompilerParams(
            collective_id=0, has_side_effects=True, vmem_limit_bytes=60 << 20
        ),
        name="main",
    )(owner_map, queries, cluster_ids.reshape(count, 1, sel), positives, panels, scales)

    return pl.pallas_call(
        output_kernel,
        out_shape=(
            sds((count, rows), bf16),
            sds((count, rows, width), bf16),
            sds((slots, 2, width), f32),
        ),
        in_specs=[hbm] * 4,
        out_specs=(hbm,) * 3,
        scratch_shapes=[
            vm((count, rows, width), bf16), vm((count, 1, rows), f32),
            vm((2, 16, 128), f32), vm((2, 16, 128), f32),
            vm((count, rows), bf16), vm((slots, 2, width), f32), dma((13,)),
        ],
        compiler_params=pltpu.CompilerParams(vmem_limit_bytes=60 << 20),
        name="write",
    )(qg, loss, fin, rfin)


def solution(mesh):
    return jax.shard_map(
        shards,
        mesh=mesh,
        in_specs=(
            P(("tower", "group", "blk"), None, None),
            P(("tower", "group", "blk"), None),
            P(("tower", "group", "blk"), None),
            P("group", None),
            P(("group", "blk"), None, None),
            P(("group", "blk"), None),
        ),
        out_specs=(
            P(("tower", "group", "blk"), None),
            P(("tower", "group", "blk"), None, None),
            P(("group", "blk"), "tower", None),
        ),
        check_vma=False,
    )
```

time: 248 us -> 55.4 us (0.22)
  waiting for transfers between devices: 113 us -> 0 us
  Pallas kernels: 0 us -> 54.6 us
  local copies, waits for them, and re-layouts: 36.1 us -> 0 us
  blocking collectives: 35.9 us -> 0 us
  starting transfers between devices: 16.8 us -> 0 us
  other arithmetic: 15.8 us -> 0 us
  matrix products: 14.6 us -> 0 us
  between operations: 13.9 us -> 0.64 us
    unnamed x4 -> x0, waiting for transfers between devices: 60 us -> none
    pallas_call x0 -> x2, Pallas kernels: none -> 54.6 us  [the longest x1 52.6 us: shards(): pl.pallas_call(main_kernel, out_shape=(sds((count, rows, width), bf16), s...]
    reduce_scatter x1 -> x0, waiting for transfers between devices: 49.6 us -> none  [shards(): lax.psum_scatter(grad_accum, 'tower', scatter_dimension=1, tiled=True)]
    all_gather x1 -> x0, blocking collectives: 29.4 us -> none  [shards(): lax.all_gather(scales, 'blk', axis=0, tiled=True)]
    all_to_all x4 -> x0, starting transfers between devices: 16.7 us -> none  [the longest x1 4.84 us: shards(): lax.all_to_all(cluster_ids, 'group', split_axis=0, concat_axis=0, tiled=T...]
    dot_general x3 -> x0, matrix products: 14.6 us -> none  [the longest x1 5.47 us: shards(): jnp.dot(weights, whole_panels.reshape(group_slots * panel_items, feat_wid...]
    gather x2 -> x0, local copies, waits for them, and re-layouts: 13.3 us -> none  [shards(): pos_slot = jnp.take_along_axis(listed, positives // panel_items, axis=1)]
    dot_general x1 -> x0, local copies, waits for them, and re-layouts: 8.63 us -> none  [shards(): jnp.dot(weights.T, flat_query, preferred_element_type=jnp.float32)]
  transfers between devices with their start and end apart: 7 -> 0, of which waited for: 3 -> 0; matrix products, arithmetic and copies ran while one was open for 12% -> 0% of each run, Pallas kernels for 0% -> 0%
where the time goes in v2:
time: 55.4 us; the launch traced here: 55.3 us
  Pallas kernels  54.6 us (99%)
  between operations  0.64 us (1%)
    pallas_call x1, Pallas kernels, shards(): pl.pallas_call(main_kernel, out_shape=(sds((count, rows, width), bf16), s...  52.6 us
    pallas_call x1, Pallas kernels, shards(): pl.pallas_call(output_kernel, out_shape=(sds((count, rows), bf16), sds((c...  2.05 us

profile of v2, /device:TPU:1, one launch (start us, length us, event | category | flops | bytes accessed | tf_op | source)
XLA Modules:
  0.0 55.3 jit_solution(3126813143501657248)
XLA Ops:
  0.6 52.6 %main.1 = (bf16[4,384,256]{2,1,0:T(8,128)(2,1)}, f32[4,1,384]{2,1,0:T(1,128)}, f32[2,16,128]{2,1,0:T(8,128)}, f32[2,16,128]{2,1,0:T(8,128)}) custom-call(s32[1,128]{1,0:T(1,128)} %owner.1, bf16[4,384,256]{2,1,0:T(8,128)(2,1)} %q.1, s32[4,1,64]{2,1,0:T(1,128)} %bitcast.1, s32[4,384]{1,0:T(4,128)} %pos.1, bf16[8,16,256]{2,1,0:T(8,128)(2,1)} %pan.1, ...), custom_call_target="tpu_custom_call" | custom-call | tf_op jit(solution)/shard_map/main/pallas_call | solution.py:380
  53.2 2.1 %write.1 = (bf16[4,384]{1,0:T(4,128)(2,1)}, bf16[4,384,256]{2,1,0:T(8,128)(2,1)}, f32[8,2,256]{2,1,0:T(2,128)}) custom-call(bf16[4,384,256]{2,1,0:T(8,128)(2,1)} %get-tuple-element.7.qg, f32[4,1,384]{2,1,0:T(1,128)} %get-tuple-element.8.loss, f32[2,16,128]{2,1,0:T(8,128)} %get-tuple-element.9.fin, f32[2,16,128]{2,1,0:T(8,128)} %get-tuple-element.10.rfin), custom_call_target="tpu_custom_call" | custom-call | tf_op jit(solution)/shard_map/write/pallas_call | solution.py:427

commit v3 on v2

--- a/solution.py
+++ b/solution.py
@@ -7,7 +7,7 @@
 
 MESH = pl.DeviceIdType.MESH
 NX, NY, NZ = 4, 8, 8
-FAR_FIRST = (4, 3, 5, 2, 6, 1, 7)
+INWARD = (4, 3, 5, 2, 6, 1, 7)
 
 
 def remote(src, dst, send, recv, peer):
@@ -66,21 +66,21 @@
 
 
 def main_kernel(
-    owner, q, ids, pos, pan, sc,
-    qg_out, loss_out, fin_out, rfin,
-    qo, ido, poso, pano, sco, ids_s, tab, cand, sbuf, wbuf, gbuf, lossb, qgb, inv_v, inv_s,
-    p0, own0, r0, s0, r1, s1, r2, fin,
+    own_map, q, ids, pos, pan, sc,
+    qg_out, loss_out, pg_out,
+    owner, lbuf, qo, ido, poso, pano, sco, ids_s, tab, cand, sbuf, wbuf, gbuf, lossb, qgb, inv_v, inv_s,
+    p0, own0, r0, s0, r1, s1, r2,
     loc, xs, xr, ys, yr, yss, yrs, zs, zr, zss, zrs, ps, pr, ready1, ready2,
-    cs, cr, s1s, s1r, s2s, s2r, bs, br, fs, fr,
+    cs, cr, s1s, s1r, s2s, s2r, bs, br,
 ):
     t, g, b = lax.axis_index("tower"), lax.axis_index("group"), lax.axis_index("blk")
     core, y, zl = lax.rem(t, 2), lax.div(b, 2), lax.rem(b, 2)
     z = 2 * lax.div(t, 2) + zl
     step = 1 - 2 * core
 
-    def at_yz(yy, zz):
+    def at_yz(yy, zz, c=core):
         yy, zz = lax.rem(yy + NY, NY), lax.rem(zz + NZ, NZ)
-        return (2 * lax.div(zz, 2) + core, g, 2 * yy + lax.rem(zz, 2))
+        return (2 * lax.div(zz, 2) + c, g, 2 * yy + lax.rem(zz, 2))
 
     partner = (t + step, g, b)
     x_peers = [(t, lax.rem(g + d, NX), b) for d in range(1, NX)]
@@ -89,19 +89,23 @@
     local = [
         pltpu.make_async_copy(pan, pano.at[b], loc.at[0]),
         pltpu.make_async_copy(sc, sco.at[b], loc.at[1]),
-        pltpu.make_async_copy(q.at[g], qo.at[g], loc.at[2]),
-        pltpu.make_async_copy(ids.at[g], ido.at[g], loc.at[3]),
-        pltpu.make_async_copy(pos, poso.at[g], loc.at[4]),
+        pltpu.make_async_copy(own_map, owner, loc.at[2]),
     ]
-    near = [at_yz(y + d, z) for d in (2, -2, 1, -1)] + x_peers + [z_to, z_from, partner]
+    own = [
+        pltpu.make_async_copy(ids.at[g], ido.at[g], xr.at[0, 0]),
+        pltpu.make_async_copy(pos, poso.at[g], xr.at[0, 1]),
+        pltpu.make_async_copy(q.at[g], qo.at[g], xr.at[0, 2]),
+    ]
+    near = [at_yz(y + d, z) for d in (2, -2)] + x_peers
+    near += [at_yz(y + d, z) for d in (1, -1)] + [z_to, z_from, partner]
     barrier = pltpu.get_barrier_semaphore()
+    for d in (2 * step, 1, -1):
+        signal(barrier, at_yz(y - d, z - step))
     for peer in near:
         signal(barrier, peer)
-    for copy in local:
+    for copy in local + own:
         copy.start()
-    pl.semaphore_wait(barrier, len(near))
-    for peer in (z_to, z_from):
-        signal(ready1, peer)
+    pl.semaphore_wait(barrier, len(near) + 3)
 
     half = pl.ds(core * 4, 4)
     sends = []
@@ -114,21 +118,17 @@
 
     y_in, z_in, p_in = {}, {}, []
 
-    def y_send(d, src_blk, to_y):
-        for own, (buf, s, r) in (
-            (pan.at[half], (pano.at[src_blk, half], ys, yr)),
-            (sc, (sco.at[src_blk], yss, yrs)),
-        ):
-            src = own if src_blk is b else buf
-            y_in.setdefault(d, []).append(send(src, buf, s.at[d - 1], r.at[d - 1], at_yz(to_y, z)))
-
-    def z_send(d, src_blk):
-        for own, (buf, s, r) in (
-            (pan.at[half], (pano.at[src_blk, half], zs, zr)),
-            (sc, (sco.at[src_blk], zss, zrs)),
-        ):
-            src = own if src_blk is b else buf
-            z_in.setdefault(d, []).append(send(src, buf, s.at[d], r.at[d], z_to))
+    def y_send(d, src_blk, panel, scale, peer):
+        y_in[d] = [
+            send(panel, pano.at[src_blk, half], ys.at[d - 1], yr.at[d - 1], peer),
+            send(scale, sco.at[src_blk], yss.at[d - 1], yrs.at[d - 1], peer),
+        ]
+
+    def z_send(d, src_blk, panel, scale, peer):
+        z_in[d] = [
+            send(panel, pano.at[src_blk, half], zs.at[d], zr.at[d], peer),
+            send(scale, sco.at[src_blk], zss.at[d], zrs.at[d], peer),
+        ]
 
     def p_send(src_blk):
         k = len(p_in)
@@ -138,18 +138,20 @@
     def blk_at(d, side):
         return 2 * lax.rem(y - d + NY, NY) + side
 
-    y_send(2, b, y + 2)
-    y_send(6, b, y - 2)
-    y_send(1, b, y + 1)
-    y_send(7, b, y - 1)
-    z_send(0, b)
-    x_in = []
-    for d in (2, 1, 3):
+    for d in (2, 6, 1, 7):
+        y_send(d, b, pan.at[half], sc, at_yz(y + d, z))
+    z_send(0, b, pan.at[half], sc, z_to)
+    for peer in (z_to, z_from):
+        signal(ready1, peer)
+    ids_in = []
+    for d in (1, 3, 2):
         dst = lax.rem(g + d, NX)
         for n, (src, out) in enumerate(
             ((ids.at[dst], ido.at[g]), (pos, poso.at[g]), (q.at[dst], qo.at[g]))
         ):
-            x_in.append(send(src, out, xs.at[d - 1, n], xr.at[d - 1, n], x_peers[d - 1]))
+            copy = send(src, out, xs.at[d - 1, n], xr.at[d, n], x_peers[d - 1])
+            if n == 0:
+                ids_in.append(copy)
 
     def take_y(d):
         for copy in y_in[d]:
@@ -160,35 +162,39 @@
             copy.wait_recv()
         p_send(blk_at(d, 1 - zl))
 
+    def pass_on(d, src, dy):
+        panel, scale = pano.at[src, half], sco.at[src]
+        z_send(d, src, panel, scale, at_yz(y + dy, z + step))
+        y_send(d, src, panel, scale, at_yz(y + dy, z))
+
+    def spread(d):
+        src = blk_at(d, zl)
+        z_send(d, src, pano.at[src, half], sco.at[src], z_to)
+        p_send(src)
+
+    take_y(2)
+    pass_on(3, blk_at(2, zl), 1)
+    take_y(6)
+    pass_on(5, blk_at(6, zl), -1)
+    pass_on(4, 2 * lax.rem(y - 2 * step + NY, NY) + zl, 2 * step)
     for d in (1, 7):
         take_y(d)
-        z_send(d, blk_at(d, zl))
-        p_send(blk_at(d, zl))
-    take_y(2)
-    y_send(3, blk_at(2, zl), y + 1)
-    take_y(6)
-    y_send(5, blk_at(6, zl), y - 1)
-    y_send(4, 2 * lax.rem(y - 2 * step + NY, NY) + zl, y + 2 * step)
-    for d in (2, 6):
-        z_send(d, blk_at(d, zl))
-        p_send(blk_at(d, zl))
+    for d in (2, 6, 1, 7):
+        spread(d)
     take_z(0)
     pl.semaphore_wait(ready1, 2)
     for d in (2, -2):
         signal(ready2, at_yz(y, z + d))
-    take_z(1)
-    take_z(7)
     for d in (3, 5, 4):
         take_y(d)
-        z_send(d, blk_at(d, zl))
         p_send(blk_at(d, zl))
-    for d in (2, 6, 3, 5, 4):
+    for d in (1, 7, 2, 6, 3, 5, 4):
         take_z(d)
-    for copy in local:
+    for copy in local + own[:1]:
         copy.wait()
-    for copy in x_in:
+    for copy in ids_in:
         copy.wait_recv()
-    to_smem = pltpu.make_async_copy(ido, ids_s, loc.at[5])
+    to_smem = pltpu.make_async_copy(ido, ids_s, loc.at[3])
     to_smem.start()
 
     items = 16
@@ -208,7 +214,11 @@
     to_smem.wait()
     lane = lax.broadcasted_iota(jnp.int32, (1, 128), 1)
 
-    def block(n, carry):
+    def block(k, carry):
+        d = k + lax.div(k, 2) * (5 - 2 * k)
+        n = lax.rem(g - d + NX, NX)
+        pltpu.make_async_copy(pos, poso.at[n], xr.at[d, 1]).wait()
+        pltpu.make_async_copy(q.at[n], qo.at[n], xr.at[d, 2]).wait()
         slots = [owner[0, ids_s[n, 0, j]] for j in range(sel)]
         where = jnp.full((1, 128), sel, jnp.int32)
         for j in range(sel):
@@ -218,7 +228,7 @@
         return carry
 
     lax.fori_loop(0, NX, block, 0)
-    inv_copy = pltpu.make_async_copy(inv_v, inv_s, loc.at[6])
+    inv_copy = pltpu.make_async_copy(inv_v, inv_s, loc.at[4])
     inv_copy.start()
     inv_copy.wait()
 
@@ -255,18 +265,18 @@
         return carry
 
     firsts = []
+    pl.semaphore_wait(ready2, 2)
     lax.fori_loop(0, NY, pack_away, 0)
     for f in range(2):
         firsts.append(send(p0.at[f], r0.at[f], cs.at[f], cr.at[f], partner))
     lax.fori_loop(0, NY, pack_own, 0)
-    pl.semaphore_wait(ready2, 2)
     here = (y, z)
     ahead = (lambda d: at_yz(y + d, z), lambda d: at_yz(y, z + d))
     stage1 = ([], [])
 
     for f in range(2):
         firsts[f].wait_recv()
-    for d in FAR_FIRST + (0,):
+    for d in INWARD + (0,):
         for f in range(2):
             k = lax.rem(here[f] + d, 8)
             s0[f, k] = (own0[f, k] + r0[f, k].astype(jnp.float32)).astype(jnp.bfloat16)
@@ -283,18 +293,18 @@
 
     lax.fori_loop(0, NX, back, 0)
     home = [
-        pltpu.make_async_copy(qgb.at[g], qg_out.at[g], loc.at[7]),
-        pltpu.make_async_copy(lossb.at[g], loss_out.at[g], loc.at[8]),
+        pltpu.make_async_copy(qgb.at[g], qg_out.at[g], loc.at[5]),
+        pltpu.make_async_copy(lossb.at[g], lbuf.at[g], loc.at[6]),
     ]
     backs = []
     for d in (2, 1, 3):
         dst = lax.rem(g + d, NX)
-        for n, (src, out) in enumerate(((lossb, loss_out), (qgb, qg_out))):
+        for n, (src, out) in enumerate(((lossb, lbuf), (qgb, qg_out))):
             backs.append(send(src.at[dst], out.at[g], bs.at[d - 1, n], br.at[d - 1, n], x_peers[d - 1]))
     for copy in home:
         copy.start()
 
-    stage2 = ([], [])
+    stage2 = []
     for f in range(2):
         for copy in stage1[f]:
             copy.wait_recv()
@@ -302,26 +312,32 @@
         for d in range(7):
             total = total + r1[f, d].astype(jnp.float32)
         s1[f] = total.astype(jnp.bfloat16)
-        for d in FAR_FIRST:
-            k = lax.rem(here[1 - f] + d, 8)
-            stage2[f].append(
-                send(s1.at[f, k], r2.at[f, d - 1], s2s.at[f, d - 1], s2r.at[f, d - 1], ahead[1 - f](d))
-            )
-    for f in range(2):
-        for copy in stage2[f]:
-            copy.wait_recv()
-        total = s1[f, here[1 - f]].astype(jnp.float32)
-        for d in range(7):
-            total = total + r2[f, d].astype(jnp.float32)
-        fin[f] = total
-    last = send(fin, rfin, fs, fr, partner)
-    home.append(pltpu.make_async_copy(fin, fin_out, loc.at[9]))
-    home[-1].start()
+        for d in INWARD + (0,):
+            piece = s1.at[f, lax.rem(here[1 - f] + d, 8)]
+            for other in (1, 0) if d else (1,):
+                c = core + other * step
+                peer = at_yz(y, z + d, c) if f == 0 else at_yz(y + d, z, c)
+                stage2.append(
+                    send(piece, r2.at[core, f, d], s2s.at[other, f, d], s2r.at[other, f, d], peer)
+                )
+    r2[core, 0, 0] = s1[0, z]
+    r2[core, 1, 0] = s1[1, y]
     for copy in home:
         copy.wait()
     for copy in backs:
         copy.wait_recv()
-    last.wait_recv()
+    for n in range(NX):
+        loss_out[n : n + 1, :] = lbuf[n].astype(jnp.bfloat16)
+    for copy in stage2:
+        copy.wait_recv()
+    for h in range(2):
+        for f in range(2):
+            tile = r2[h, f, 0].astype(jnp.float32)
+            for d in range(1, 8):
+                tile = tile + r2[h, f, d].astype(jnp.float32)
+            for k in range(4):
+                rows = jnp.where(core == 0, tile[4 * k : 4 * k + 2], tile[4 * k + 2 : 4 * k + 4])
+                pg_out[4 * h + k, :, 128 * f : 128 * f + 128] = rows
     for copy in sends:
         copy.wait_send()
 
@@ -330,37 +346,14 @@
     return ref.reshape(ref.shape[0] * ref.shape[1], *ref.shape[2:])
 
 
-def output_kernel(qg, loss, fin, rfin, loss_out, qg_out, pg_out, qv, lv, fv, rv, lossv, pgv, sem):
-    small = [
+def output_kernel(loss, qg, pg, loss_out, qg_out, pg_out, sem):
+    copies = [
         pltpu.make_async_copy(src, dst, sem.at[n])
-        for n, (src, dst) in enumerate(((loss, lv), (fin, fv), (rfin, rv)))
+        for n, (src, dst) in enumerate(((qg, qg_out), (loss, loss_out), (pg, pg_out)))
     ]
-    taken = [pltpu.make_async_copy(qg.at[n], qv.at[n], sem.at[3 + n]) for n in range(NX)]
-    for copy in small + taken:
+    for copy in copies:
         copy.start()
-    given = []
-    for copy in small:
-        copy.wait()
-    core = lax.rem(lax.axis_index("tower"), 2)
-    for n in range(NX):
-        lossv[n : n + 1, :] = lv[n].astype(jnp.bfloat16)
-    for h in range(2):
-        for f in range(2):
-            tile = jnp.where(core == h, fv[f], rv[f])
-            for k in range(4):
-                rows = jnp.where(core == 0, tile[4 * k : 4 * k + 2], tile[4 * k + 2 : 4 * k + 4])
-                pgv[4 * h + k, :, 128 * f : 128 * f + 128] = rows
-    given = [
-        pltpu.make_async_copy(lossv, loss_out, sem.at[7]),
-        pltpu.make_async_copy(pgv, pg_out, sem.at[8]),
-    ]
-    for copy in given:
-        copy.start()
-    for n in range(NX):
-        taken[n].wait()
-        given.append(pltpu.make_async_copy(qv.at[n], qg_out.at[n], sem.at[9 + n]))
-        given[-1].start()
-    for copy in given:
+    for copy in copies:
         copy.wait()
 
 
@@ -377,17 +370,20 @@
     sds = jax.ShapeDtypeStruct
     vm = pltpu.VMEM
 
-    qg, loss, fin, rfin = pl.pallas_call(
+    args = (owner_map, queries, cluster_ids.reshape(count, 1, sel), positives, panels, scales)
+    outs = (
+        sds((count, rows), bf16),
+        sds((count, rows, width), bf16),
+        sds((slots, 2, width), f32),
+    )
+    qg, loss, pg = pl.pallas_call(
         main_kernel,
-        out_shape=(
-            sds((count, rows, width), bf16),
-            sds((count, 1, rows), f32),
-            sds((2, 16, 128), f32),
-            sds((2, 16, 128), f32),
-        ),
-        in_specs=[smem] + [hbm] * 5,
-        out_specs=(hbm,) * 4,
+        out_shape=(outs[1], outs[0], outs[2]),
+        in_specs=[hbm] * 6,
+        out_specs=(vmem,) * 3,
         scratch_shapes=[
+            pltpu.SMEM(owner_map.shape, i32),
+            vm((count, 1, rows), f32),
             vm((count, rows, width), bf16),
             vm((count, 1, sel), i32),
             vm((count, count, rows), i32),
@@ -409,38 +405,29 @@
             vm((2, 8, 8, 16, 128), bf16),
             vm((2, 7, 8, 16, 128), bf16),
             vm((2, 8, 16, 128), bf16),
-            vm((2, 7, 16, 128), bf16),
-            vm((2, 16, 128), f32),
-            dma((10,)), dma((3, 3)), dma((3, 3)),
+            vm((2, 2, 8, 16, 128), bf16),
+            dma((7,)), dma((3, 3)), dma((4, 3)),
             dma((7,)), dma((7,)), dma((7,)), dma((7,)),
             dma((8,)), dma((8,)), dma((8,)), dma((8,)), dma((15,)), dma((15,)),
             pltpu.SemaphoreType.REGULAR, pltpu.SemaphoreType.REGULAR,
-            dma((2,)), dma((2,)), dma((2, 7)), dma((2, 7)), dma((2, 7)), dma((2, 7)),
-            dma((3, 2)), dma((3, 2)), dma, dma,
+            dma((2,)), dma((2,)), dma((2, 7)), dma((2, 7)), dma((2, 2, 8)), dma((2, 2, 8)),
+            dma((3, 2)), dma((3, 2)),
         ],
         compiler_params=pltpu.CompilerParams(
-            collective_id=0, has_side_effects=True, vmem_limit_bytes=60 << 20
+            collective_id=0, has_side_effects=True, vmem_limit_bytes=40 << 20
         ),
         name="main",
-    )(owner_map, queries, cluster_ids.reshape(count, 1, sel), positives, panels, scales)
+    )(*[pltpu.with_memory_space_constraint(arg, pltpu.HBM) for arg in args])
 
     return pl.pallas_call(
         output_kernel,
-        out_shape=(
-            sds((count, rows), bf16),
-            sds((count, rows, width), bf16),
-            sds((slots, 2, width), f32),
-        ),
-        in_specs=[hbm] * 4,
+        out_shape=outs,
+        in_specs=[vmem] * 3,
         out_specs=(hbm,) * 3,
-        scratch_shapes=[
-            vm((count, rows, width), bf16), vm((count, 1, rows), f32),
-            vm((2, 16, 128), f32), vm((2, 16, 128), f32),
-            vm((count, rows), bf16), vm((slots, 2, width), f32), dma((13,)),
-        ],
-        compiler_params=pltpu.CompilerParams(vmem_limit_bytes=60 << 20),
+        scratch_shapes=[dma((3,))],
+        compiler_params=pltpu.CompilerParams(vmem_limit_bytes=4 << 20),
         name="write",
-    )(qg, loss, fin, rfin)
+    )(loss, qg, pg)
 
 
 def solution(mesh):

time: 55.4 us -> 50.9 us (0.919)
  Pallas kernels: 54.6 us -> 50.2 us
    pallas_call x2, Pallas kernels: 54.6 us -> 50.2 us  [the longest x1 49.2 us: shards(): pl.pallas_call(main_kernel, out_shape=(outs[1], outs[0], outs[2]), in_spe...]
where the time goes in v3:
time: 50.9 us; the launch traced here: 50.8 us
  Pallas kernels  50.2 us (99%)
  between operations  0.64 us (1%)
    pallas_call x1, Pallas kernels, shards(): pl.pallas_call(main_kernel, out_shape=(outs[1], outs[0], outs[2]), in_spe...  49.2 us

profile of v3, /device:TPU:1, one launch (start us, length us, event | category | flops | bytes accessed | tf_op | source)
XLA Modules:
  0.0 50.8 jit_solution(3423338790019477510)
XLA Ops:
  0.6 49.2 %main.1 = (bf16[4,384,256]{2,1,0:T(8,128)(2,1)S(1)}, bf16[4,384]{1,0:T(4,128)(2,1)S(1)}, f32[8,2,256]{2,1,0:T(2,128)S(1)}) custom-call(s32[1,128]{1,0:T(1,128)} %own_map.1, bf16[4,384,256]{2,1,0:T(8,128)(2,1)} %q.1, s32[4,1,64]{2,1,0:T(1,128)} %bitcast.1, s32[4,384]{1,0:T(4,128)} %pos.1, bf16[8,16,256]{2,1,0:T(8,128)(2,1)} %pan.1, bf16[8,16]{1,0:T(8,128)(2,1)} %sc.1), custom_call_target="tpu_custom_call" | custom-call | tf_op jit(solution)/shard_map/main/pallas_call | solution.py:379
  49.9 0.9 %write.1 = (bf16[4,384]{1,0:T(4,128)(2,1)}, bf16[4,384,256]{2,1,0:T(8,128)(2,1)}, f32[8,2,256]{2,1,0:T(2,128)}) custom-call(bf16[4,384]{1,0:T(4,128)(2,1)S(1)} %get-tuple-element.6.loss, bf16[4,384,256]{2,1,0:T(8,128)(2,1)S(1)} %get-tuple-element.7.qg, f32[8,2,256]{2,1,0:T(2,128)S(1)} %get-tuple-element.8.pg), custom_call_target="tpu_custom_call" | custom-call | tf_op jit(solution)/shard_map/write/pallas_call | solution.py:422

commit v4 on v3

--- a/solution.py
+++ b/solution.py
@@ -153,6 +153,17 @@
             if n == 0:
                 ids_in.append(copy)
 
+    items = 16
+    eye = (
+        lax.broadcasted_iota(jnp.int32, (items, items), 0)
+        == lax.broadcasted_iota(jnp.int32, (items, items), 1)
+    ).astype(jnp.float32)
+
+    def scale_tiles(src):
+        part = sco[src].astype(jnp.float32)
+        column = jnp.sum(part[:, None, :] * eye[None], axis=2, keepdims=True)
+        tab[pl.ds(8 * src, 8)] = jnp.broadcast_to(column, (8, items, 128))
+
     def take_y(d):
         for copy in y_in[d]:
             copy.wait_recv()
@@ -161,6 +172,7 @@
         for copy in z_in[d]:
             copy.wait_recv()
         p_send(blk_at(d, 1 - zl))
+        scale_tiles(blk_at(d, 1 - zl))
 
     def pass_on(d, src, dy):
         panel, scale = pano.at[src, half], sco.at[src]
@@ -181,6 +193,13 @@
         take_y(d)
     for d in (2, 6, 1, 7):
         spread(d)
+    sel = ids_s.shape[2]
+    for n in range(NX):
+        gbuf[n, sel] = jnp.zeros(gbuf.shape[2:], jnp.float32)
+    for copy in local:
+        copy.wait()
+    for d in (0, 2, 6, 1, 7):
+        scale_tiles(blk_at(d, zl))
     take_z(0)
     pl.semaphore_wait(ready1, 2)
     for d in (2, -2):
@@ -188,27 +207,15 @@
     for d in (3, 5, 4):
         take_y(d)
         p_send(blk_at(d, zl))
-    for d in (1, 7, 2, 6, 3, 5, 4):
-        take_z(d)
-    for copy in local + own[:1]:
-        copy.wait()
+        scale_tiles(blk_at(d, zl))
+    own[0].wait()
     for copy in ids_in:
         copy.wait_recv()
     to_smem = pltpu.make_async_copy(ido, ids_s, loc.at[3])
     to_smem.start()
-
-    items = 16
-    eye = (
-        lax.broadcasted_iota(jnp.int32, (items, items), 0)
-        == lax.broadcasted_iota(jnp.int32, (items, items), 1)
-    ).astype(jnp.float32)
-    for n in range(sco.shape[0]):
-        part = sco[n].astype(jnp.float32)
-        column = jnp.sum(part[:, None, :] * eye[None], axis=2, keepdims=True)
-        tab[pl.ds(8 * n, 8)] = jnp.broadcast_to(column, (8, items, 128))
-    sel = ids_s.shape[2]
-    for n in range(NX):
-        gbuf[n, sel] = jnp.zeros(gbuf.shape[2:], jnp.float32)
+    for d in (1, 7, 2, 6, 3, 5, 4):
+        take_z(d)
+
     for copy in p_in:
         copy.wait_recv()
     to_smem.wait()
@@ -266,16 +273,21 @@
 
     firsts = []
     pl.semaphore_wait(ready2, 2)
-    lax.fori_loop(0, NY, pack_away, 0)
+    lax.fori_loop(0, NY // 2, pack_away, 0)
     for f in range(2):
-        firsts.append(send(p0.at[f], r0.at[f], cs.at[f], cr.at[f], partner))
+        part = (f, pl.ds(0, 4)) if f == 0 else (f, slice(None), pl.ds(0, 4))
+        firsts.append(send(p0.at[part], r0.at[part], cs.at[f], cr.at[f], partner))
+    lax.fori_loop(NY // 2, NY, pack_away, 0)
+    for f in range(2):
+        part = (f, pl.ds(4, 4)) if f == 0 else (f, slice(None), pl.ds(4, 4))
+        firsts.append(send(p0.at[part], r0.at[part], cs.at[2 + f], cr.at[2 + f], partner))
     lax.fori_loop(0, NY, pack_own, 0)
     here = (y, z)
     ahead = (lambda d: at_yz(y + d, z), lambda d: at_yz(y, z + d))
     stage1 = ([], [])
 
-    for f in range(2):
-        firsts[f].wait_recv()
+    for copy in firsts:
+        copy.wait_recv()
     for d in INWARD + (0,):
         for f in range(2):
             k = lax.rem(here[f] + d, 8)
@@ -410,7 +422,7 @@
             dma((7,)), dma((7,)), dma((7,)), dma((7,)),
             dma((8,)), dma((8,)), dma((8,)), dma((8,)), dma((15,)), dma((15,)),
             pltpu.SemaphoreType.REGULAR, pltpu.SemaphoreType.REGULAR,
-            dma((2,)), dma((2,)), dma((2, 7)), dma((2, 7)), dma((2, 2, 8)), dma((2, 2, 8)),
+            dma((4,)), dma((4,)), dma((2, 7)), dma((2, 7)), dma((2, 2, 8)), dma((2, 2, 8)),
             dma((3, 2)), dma((3, 2)),
         ],
         compiler_params=pltpu.CompilerParams(

time: 50.9 us -> 50.7 us (level)
  no operation moved by 1% of the time
where the time goes in v4:
time: 50.7 us; the launch traced here: 50.6 us
  Pallas kernels  49.9 us (98%)
  between operations  0.64 us (1%)
    pallas_call x1, Pallas kernels, shards(): pl.pallas_call(main_kernel, out_shape=(outs[1], outs[0], outs[2]), in_spe...  49 us

profile of v4, /device:TPU:1, one launch (start us, length us, event | category | flops | bytes accessed | tf_op | source)
XLA Modules:
  0.0 50.6 jit_solution(5180379432961125166)
XLA Ops:
  0.6 49.0 %main.1 = (bf16[4,384,256]{2,1,0:T(8,128)(2,1)S(1)}, bf16[4,384]{1,0:T(4,128)(2,1)S(1)}, f32[8,2,256]{2,1,0:T(2,128)S(1)}) custom-call(s32[1,128]{1,0:T(1,128)} %own_map.1, bf16[4,384,256]{2,1,0:T(8,128)(2,1)} %q.1, s32[4,1,64]{2,1,0:T(1,128)} %bitcast.1, s32[4,384]{1,0:T(4,128)} %pos.1, bf16[8,16,256]{2,1,0:T(8,128)(2,1)} %pan.1, bf16[8,16]{1,0:T(8,128)(2,1)} %sc.1), custom_call_target="tpu_custom_call" | custom-call | tf_op jit(solution)/shard_map/main/pallas_call | solution.py:391
  49.7 0.9 %write.1 = (bf16[4,384]{1,0:T(4,128)(2,1)}, bf16[4,384,256]{2,1,0:T(8,128)(2,1)}, f32[8,2,256]{2,1,0:T(2,128)}) custom-call(bf16[4,384]{1,0:T(4,128)(2,1)S(1)} %get-tuple-element.6.loss, bf16[4,384,256]{2,1,0:T(8,128)(2,1)S(1)} %get-tuple-element.7.qg, f32[8,2,256]{2,1,0:T(2,128)S(1)} %get-tuple-element.8.pg), custom_call_target="tpu_custom_call" | custom-call | tf_op jit(solution)/shard_map/write/pallas_call | solution.py:434
